TPU v7x, 256 devices: a whole 4x4x8 slice. The times are simulated.
256 devices in a mesh: ctx: 32 (over z, x_hi, core), head: 8 (over y, x_lo).
Axes of the slice: x: 4 (x_hi: 2, x_lo: 2; x = x_hi * 2 + x_lo), y: 4, z: 8, core: 2. Of those that a mesh axis runs over, the one named last changes fastest.
Arguments:
- queries: bfloat16 [8192, 8192], P('ctx', 'head'), may hold values from -10 to 10
- key_rows: bfloat16 [8192, 1024], P('ctx', 'head'), may hold values from -4.5 to 4.5
- values: bfloat16 [8192, 1024], P('ctx', 'head'), may hold values from -24 to 24
- lengths: int32 [17], replicated, may hold values from 1 to 4352, as said below
- block_plan: int32 [1024], P('ctx'), may hold values from 0 to 1023, as said below
- inverse: int32 [1024], replicated, may hold values from 0 to 1023, as said below
- mask_lo: int32 [1024], replicated, may hold values from 0 to 1023, as said below
- out_weight: bfloat16 [8192, 4096], P('head'), may hold values from -0.375 to 0.375
Outputs:
- mixed_out: bfloat16 [8192, 4096], P('ctx', 'head')
Inputs may be any that keep to these rules, and one draw needn't show every extreme that they name: One document has exactly 4352 tokens, every other is shorter; the lengths sum to 8192. A permutation of the 1024 blocks; slot block_plan[b] lies on index block_plan[b] // 32 of ctx; every index receives exactly 32 blocks, and at most 2 blocks of one index go to any one index, which is reached in every draw. inverse[block_plan[b]] == b. mask_lo[b] lies between the block holding the first token of the document of block b's first token and b, both included.
All inputs are finite; a program needn't handle non-finite values.
Results may differ from a plain program's by a relative error of at most 0.02.
Values may be sent and summed in bfloat16 or wider, within the bound.
A program may use at most 64 MiB of HBM per device.

v0:
```python
import functools

import jax
import jax.numpy as jnp
from jax import lax
from jax.experimental import pallas as pl
from jax.experimental.pallas import tpu as pltpu
from jax.sharding import PartitionSpec as P

HD = 128
BLK = 8
TQ = 1024
TK = 512
SHARD = 256
NEG_FILL = -1e30
LONGEST = 4352
PLANE = 4


def attn_kernel(plane, slots, tiles_ref, q_ref, kv_ref, qpos_ref, lo_ref, o_ref, m_sc, l_sc, acc_sc):
    n_q = q_ref.shape[0] * q_ref.shape[1] // (HD * TQ)
    scale = HD ** (-0.5)

    def q_body(qi, carry):
        r0 = pl.multiple_of(qi * TQ, TQ)
        heads = TQ // q_ref.shape[0]
        q = jnp.concatenate([
            q_ref[:, pl.ds(pl.multiple_of((qi * heads + g) * HD, HD), HD)] for g in range(heads)
        ], axis=0)
        qpos = qpos_ref[:, pl.ds(r0, TQ)]
        lo = lo_ref[:, pl.ds(r0, TQ)]
        m_sc[...] = jnp.full(m_sc.shape, NEG_FILL, jnp.float32)
        l_sc[...] = jnp.zeros(l_sc.shape, jnp.float32)
        acc_sc[...] = jnp.zeros(acc_sc.shape, jnp.float32)

        def k_step(kj, masked):
            c0 = pl.multiple_of(kj * TK, TK)
            at = []
            for piece in range(TK // SHARD):
                i = kj * (TK // SHARD) + piece
                at.append(pl.multiple_of((lax.rem(i, plane) * slots + i // plane) * 2 * SHARD, SHARD))
            s = jnp.concatenate([
                lax.dot_general(
                    kv_ref[pl.ds(a, SHARD), :], q, (((1,), (1,)), ((), ())),
                    preferred_element_type=jnp.float32,
                )
                for a in at
            ], axis=0) * scale
            if masked:
                kpos = c0 + lax.broadcasted_iota(jnp.int32, (TK, TQ), 0)
                ok = (kpos >= lo) & (kpos <= qpos)
                s = jnp.where(ok, s, NEG_FILL)
            m_prev = m_sc[...]
            m_new = jnp.maximum(m_prev, jnp.max(s, axis=0, keepdims=True))
            p = jnp.exp(s - m_new)
            if masked:
                p = jnp.where(ok, p, 0.0)
            fade = jnp.exp(m_prev - m_new)
            l_sc[...] = l_sc[...] * fade + jnp.sum(p, axis=0, keepdims=True)
            pb = p.astype(jnp.bfloat16)
            update = acc_sc[...] * fade
            for piece, a in enumerate(at):
                update = update + lax.dot_general(
                    kv_ref[pl.ds(a + SHARD, SHARD), :], pb[piece * SHARD:(piece + 1) * SHARD],
                    (((0,), (0,)), ((), ())), preferred_element_type=jnp.float32,
                )
            acc_sc[...] = update
            m_sc[...] = m_new

        def masked_body(kj, c):
            k_step(kj, True)
            return c

        def open_body(kj, c):
            k_step(kj, False)
            return c

        lax.fori_loop(tiles_ref[qi, 0], tiles_ref[qi, 1], masked_body, 0)
        lax.fori_loop(tiles_ref[qi, 1], tiles_ref[qi, 2], open_body, 0)
        lax.fori_loop(tiles_ref[qi, 2], tiles_ref[qi, 3], masked_body, 0)
        out = (acc_sc[...] / l_sc[...]).T.astype(o_ref.dtype)
        tokens = q_ref.shape[0]
        for g in range(heads):
            o_ref[:, pl.ds(pl.multiple_of((qi * heads + g) * HD, HD), HD)] = out[g * tokens:(g + 1) * tokens]
        return carry

    lax.fori_loop(0, n_q, q_body, 0)


def attend(q_rows, kv_all, qpos_rows, lo_rows, tiles, plane, slots):
    vmem = pltpu.MemorySpace.VMEM if hasattr(pltpu, "MemorySpace") else pltpu.VMEM
    return pl.pallas_call(
        functools.partial(attn_kernel, plane, slots),
        out_shape=jax.ShapeDtypeStruct(q_rows.shape, jnp.bfloat16),
        in_specs=[
            pl.BlockSpec(memory_space=pltpu.SMEM),
            pl.BlockSpec(memory_space=vmem),
            pl.BlockSpec(memory_space=vmem),
            pl.BlockSpec(memory_space=vmem),
            pl.BlockSpec(memory_space=vmem),
        ],
        out_specs=pl.BlockSpec(memory_space=vmem),
        scratch_shapes=[
            pltpu.VMEM((1, TQ), jnp.float32),
            pltpu.VMEM((1, TQ), jnp.float32),
            pltpu.VMEM((HD, TQ), jnp.float32),
        ],
    )(tiles, q_rows, kv_all, qpos_rows, lo_rows)


MESH_ID = pl.DeviceIdType.MESH


def window_kernel(depth, plane, n_ctx, need_col, k_ref, v_ref, win_ref, send1, recv1, send2, recv2, local_sem):
    me = lax.axis_index("ctx")
    h = lax.axis_index("head")
    z = me // plane
    r = me % plane
    n_z = n_ctx // plane
    mate = r + 1 - 2 * (r % 2)
    across = (r + 2) % plane
    far = across + 1 - 2 * (across % 2)
    barrier = pltpu.get_barrier_semaphore()

    @pl.when(z + 1 < n_z)
    def _():
        pl.semaphore_signal(barrier, 1, device_id=(me + plane, h), device_id_type=MESH_ID)

    @pl.when(z - 1 >= 0)
    def _():
        pl.semaphore_signal(barrier, 1, device_id=(me - plane, h), device_id_type=MESH_ID)

    for peer in (mate, across):
        pl.semaphore_signal(barrier, 1, device_id=(z * plane + peer, h), device_id_type=MESH_ID)
    pl.semaphore_wait(barrier, jnp.minimum(1, n_z - 1 - z) + jnp.minimum(1, z) + 2)
    local = [
        pltpu.make_async_copy(src, win_ref.at[r, depth, part], local_sem.at[part])
        for part, src in enumerate((k_ref, v_ref))
    ]
    for c in local:
        c.start()

    def wanted(d):
        return (d < depth) | (r >= need_col)

    def up(k):
        if k == 1:
            return [
                pltpu.make_async_remote_copy(
                    src_ref=src,
                    dst_ref=win_ref.at[r, depth - 1, part],
                    send_sem=send1.at[part * depth],
                    recv_sem=recv1.at[part * depth],
                    device_id=(me + plane, h),
                    device_id_type=MESH_ID,
                )
                for part, src in enumerate((k_ref, v_ref))
            ]
        return [pltpu.make_async_remote_copy(
            src_ref=win_ref.at[r, depth - k + 1],
            dst_ref=win_ref.at[r, depth - k],
            send_sem=send1.at[k - 1],
            recv_sem=recv1.at[k - 1],
            device_id=(me + plane, h),
            device_id_type=MESH_ID,
        )]

    def sends(k):
        return (z + 1 < n_z) & (z - (k - 1) >= 0) & wanted(k)

    def gets(k):
        return (z - k >= 0) & wanted(k)

    @pl.when(sends(1))
    def _():
        for c in up(1):
            c.start()

    def has(slot, col):
        return (z - (depth - slot) >= 0) & ((slot > 0) | (col >= need_col))

    def hop(idx, col, slot, to):
        return pltpu.make_async_remote_copy(
            src_ref=win_ref.at[col, slot],
            dst_ref=win_ref.at[col, slot],
            send_sem=send2.at[idx, slot],
            recv_sem=recv2.at[idx, slot],
            device_id=(z * plane + to, h),
            device_id_type=MESH_ID,
        )

    for c in local:
        c.wait()
    hop(0, r, depth, mate).start()
    hop(1, r, depth, across).start()
    for k in range(1, depth + 1):
        @pl.when(gets(k))
        def _():
            for c in up(k):
                c.wait_recv()
            hop(0, r, depth - k, mate).start()
            hop(1, r, depth - k, across).start()

        if k < depth:
            @pl.when(sends(k + 1))
            def _():
                for c in up(k + 1):
                    c.start()

    for k in range(1, depth + 1):
        @pl.when(sends(k))
        def _():
            for c in up(k):
                c.wait_send()

    for slot in range(depth, -1, -1):
        @pl.when(has(slot, across))
        def _():
            hop(1, across, slot, across).wait_recv()
            hop(2, across, slot, mate).start()

    for slot in range(depth + 1):
        @pl.when(has(slot, r))
        def _():
            hop(0, r, slot, mate).wait_send()
            hop(1, r, slot, across).wait_send()

        @pl.when(has(slot, across))
        def _():
            hop(2, across, slot, mate).wait_send()

        @pl.when(has(slot, mate))
        def _():
            hop(0, mate, slot, mate).wait_recv()

        @pl.when(has(slot, far))
        def _():
            hop(2, far, slot, mate).wait_recv()


def gather_window(key_rows, values, depth, plane, n_ctx, need_col):
    rows, width = key_rows.shape
    return pl.pallas_call(
        functools.partial(window_kernel, depth, plane, n_ctx, need_col),
        out_shape=jax.ShapeDtypeStruct((plane, depth + 1, 2, rows, width), key_rows.dtype),
        in_specs=[pl.BlockSpec(memory_space=pl.ANY)] * 2,
        out_specs=pl.BlockSpec(memory_space=pl.ANY),
        scratch_shapes=[
            pltpu.SemaphoreType.DMA((depth + 1,)),
            pltpu.SemaphoreType.DMA((depth + 1,)),
            pltpu.SemaphoreType.DMA((3, depth + 1)),
            pltpu.SemaphoreType.DMA((3, depth + 1)),
            pltpu.SemaphoreType.DMA((2,)),
        ],
        compiler_params=pltpu.CompilerParams(collective_id=0, has_side_effects=True),
    )(key_rows, values)


def project_kernel(n_head, att_ref, w_hbm, o_ref, w_buf, w_sem, send_buf, got, send_sem, recv_sem):
    me = lax.axis_index("head")
    row = lax.axis_index("ctx")
    cols = o_ref.shape[1]
    for d in list(range(1, n_head)) + [0]:
        pltpu.make_async_copy(
            w_hbm.at[:, pl.ds(pl.multiple_of(lax.rem(me + d, n_head) * cols, cols), cols)],
            w_buf.at[d], w_sem.at[d],
        ).start()
    barrier = pltpu.get_barrier_semaphore()
    for d in range(1, n_head):
        pl.semaphore_signal(
            barrier, 1, device_id=(row, lax.rem(me + d, n_head)), device_id_type=MESH_ID
        )
    pl.semaphore_wait(barrier, n_head - 1)

    def fetch(d):
        c0 = pl.multiple_of(lax.rem(me + d, n_head) * cols, cols)
        return pltpu.make_async_copy(w_hbm.at[:, pl.ds(c0, cols)], w_buf.at[d], w_sem.at[d])

    def part(d):
        fetch(d).wait()
        return jnp.dot(
            att_ref[...], w_buf[d], preferred_element_type=jnp.float32
        ).astype(jnp.bfloat16)

    def send(d):
        dst = lax.rem(me + d, n_head)
        return pltpu.make_async_remote_copy(
            src_ref=send_buf.at[d - 1],
            dst_ref=got.at[me],
            send_sem=send_sem.at[d - 1],
            recv_sem=recv_sem.at[d - 1],
            device_id=(row, dst),
            device_id_type=MESH_ID,
        )

    def arrival(d):
        src = lax.rem(me + n_head - d, n_head)
        return pltpu.make_async_remote_copy(
            src_ref=send_buf.at[d - 1],
            dst_ref=got.at[src],
            send_sem=send_sem.at[d - 1],
            recv_sem=recv_sem.at[d - 1],
            device_id=(row, src),
            device_id_type=MESH_ID,
        )

    send_buf[0] = part(1)
    for d in range(1, n_head):
        if d + 1 < n_head:
            send_buf[d] = part(d + 1)
        send(d).start()
    total = part(0).astype(jnp.float32)
    for d in range(1, n_head):
        send(d).wait_send()
        arrival(d).wait_recv()
        total = total + got[lax.rem(me + n_head - d, n_head)].astype(jnp.float32)
    o_ref[...] = total.astype(o_ref.dtype)


def project(att, out_weight, n_head):
    rows = att.shape[0]
    cols = out_weight.shape[1] // n_head
    vmem = pltpu.MemorySpace.VMEM if hasattr(pltpu, "MemorySpace") else pltpu.VMEM
    return pl.pallas_call(
        functools.partial(project_kernel, n_head),
        out_shape=jax.ShapeDtypeStruct((rows, cols), jnp.bfloat16),
        in_specs=[pl.BlockSpec(memory_space=vmem), pl.BlockSpec(memory_space=pl.ANY)],
        out_specs=pl.BlockSpec(memory_space=vmem),
        scratch_shapes=[
            pltpu.VMEM((n_head, out_weight.shape[0], cols), out_weight.dtype),
            pltpu.SemaphoreType.DMA((n_head,)),
            pltpu.VMEM((n_head - 1, rows, cols), jnp.bfloat16),
            pltpu.VMEM((n_head, rows, cols), jnp.bfloat16),
            pltpu.SemaphoreType.DMA((n_head - 1,)),
            pltpu.SemaphoreType.DMA((n_head - 1,)),
        ],
        compiler_params=pltpu.CompilerParams(collective_id=1, has_side_effects=True),
    )(att, out_weight)


def on_device(queries, key_rows, values, lengths, block_plan, inverse, mask_lo, out_weight):
    row_count, query_width = queries.shape
    group_size = query_width // HD
    here = lax.axis_index("ctx")
    first = here * row_count
    pos = first + jnp.arange(row_count, dtype=jnp.int32)
    doc_ends = jnp.cumsum(lengths).astype(jnp.int32)
    doc_start = jnp.max(jnp.where(doc_ends[None, :] <= pos[:, None], doc_ends[None, :], 0), axis=1)
    block_lo = lax.dynamic_slice_in_dim(mask_lo, here * (row_count // BLK), row_count // BLK)
    lo_tok = jnp.maximum(jnp.repeat(block_lo, BLK) * BLK, doc_start)
    qpos_rows = jnp.tile(pos, group_size)[None, :]
    lo_rows = jnp.tile(lo_tok, group_size)[None, :]
    n_q = row_count * group_size // TQ
    tile_lo = jnp.full((n_q,), jnp.min(lo_tok))
    tile_hi = jnp.full((n_q,), pos[-1])
    tile_lo_max = jnp.full((n_q,), jnp.max(lo_tok))
    tile_hi_min = jnp.full((n_q,), pos[0])

    n_ctx = lax.axis_size("ctx")
    plane = PLANE
    depth = min(n_ctx // plane - 1, -(-(LONGEST - 1) // (plane * row_count)))
    need_col = max(0, -(-(plane * row_count * depth - (LONGEST - 1) - (row_count - 1)) // row_count))
    need_col = need_col // (TK // SHARD) * (TK // SHARD)
    kv_win = gather_window(key_rows, values, depth, plane, n_ctx, need_col)
    kv_win = kv_win.reshape(-1, kv_win.shape[-1])
    base = (here // plane - depth) * plane * row_count
    span = kv_win.shape[0] // 2
    t0 = (tile_lo - base) // TK
    t3 = jnp.minimum((tile_hi - base) // TK + 1, span // TK)
    t1 = jnp.clip((tile_lo_max - base + TK - 1) // TK, t0, t3)
    t2 = jnp.clip((tile_hi_min - base + 1) // TK, t1, t3)
    tiles = jnp.stack([t0, t1, t2, t3], axis=1).astype(jnp.int32)
    att = attend(queries, kv_win, qpos_rows - base, lo_rows - base, tiles, plane, depth + 1)

    return project(att, out_weight, lax.axis_size("head"))


def solution(mesh):
    in_specs = (
        P("ctx", "head"),
        P("ctx", "head"),
        P("ctx", "head"),
        P(),
        P("ctx"),
        P(),
        P(),
        P("head", None),
    )
    out_specs = P("ctx", "head")
    return jax.shard_map(
        on_device, mesh=mesh, in_specs=in_specs, out_specs=out_specs, check_vma=False
    )
```

profile of v0, /device:TPU:192, one launch (start us, length us, event | category | flops | bytes accessed | tf_op | source)
XLA Modules:
  0.0 100.7 jit_solution(17807973211525415585)
XLA Ops:
  0.0 0.8 dynamic-slice_multiply_fusion
  0.8 0.7 fusion
  2.8 0.6 copy.10
  3.4 0.7 copy.9
  4.2 0.1 reduce.8
  4.3 0.1 select_reduce_fusion
  4.4 0.1 broadcast_in_dim.24
  4.5 0.1 broadcast_in_dim.25
  4.6 0.7 maximum_reduce_fusion
  6.5 0.1 add_add_fusion
  6.6 0.6 broadcast.348.tiles_ref
  7.2 0.6 copy.11
  7.8 33.8 %shard_map.64 = bf16[4,6,2,256,128]{4,3,2,1,0:T(8,128)(2,1)} custom-call(bf16[256,128]{1,0:T(8,128)(2,1)} %k_ref.1, bf16[256,128]{1,0:T(8,128)(2,1)} %v_ref.1), custom_call_target="tpu_custom_call" | custom-call | tf_op jit(solution)/shard_map/pallas_call | solution.py:243
  41.6 26.3 %shard_map.65.att_ref = bf16[256,1024]{1,0:T(8,128)(2,1)} custom-call(s32[2,4]{1,0:T(2,128)} %broadcast.348.tiles_ref, bf16[256,1024]{1,0:T(8,128)(2,1)} %q_ref.1, bf16[12288,128]{1,0:T(8,128)(2,1)} %bitcast.16, s32[1,2048]{1,0:T(1,128)} %bitcast.17, s32[1,2048]{1,0:T(1,128)} %bitcast.18), custom_call_target="tpu_custom_call" | custom-call | tf_op jit(solution)/shard_map/pallas_call | solution.py:92
  68.0 31.0 %shard_map.66 = bf16[256,512]{1,0:T(8,128)(2,1)} custom-call(bf16[256,1024]{1,0:T(8,128)(2,1)} %shard_map.65.att_ref, bf16[1024,4096]{1,0:T(8,128)(2,1)} %w_hbm.1), custom_call_target="tpu_custom_call" | custom-call | tf_op jit(solution)/shard_map/pallas_call | solution.py:324
  99.0 1.7 %copy.13 = bf16[256,512]{1,0:T(8,128)(2,1)} copy(bf16[256,512]{1,0:T(8,128)(2,1)} %shard_map.66) | data formatting | bytes 524288
  (4 shorter events, 0.0 us)
where the time goes:
time: 102 us; the launch traced here: 101 us
  Pallas kernels  91.2 us (89%)
  local copies, waits for them, and re-layouts  5.06 us (5%)
  between operations  2.68 us (3%)
  other arithmetic  1.75 us (2%)
    pallas_call x1, Pallas kernels, gather_window(): pl.pallas_call(functools.partial(window_kernel, depth, plane, n_ctx, need...  33.8 us
    pallas_call x1, Pallas kernels, project(): pl.pallas_call(functools.partial(project_kernel, n_head), out_shape=jax.S...  31 us
    pallas_call x1, Pallas kernels, attend(): pl.pallas_call(functools.partial(attn_kernel, plane, slots), out_shape=ja...  26.3 us
    unnamed x5, local copies, waits for them, and re-layouts  2.89 us

commit v1 on v0

--- a/solution.py
+++ b/solution.py
@@ -27,8 +27,8 @@
         q = jnp.concatenate([
             q_ref[:, pl.ds(pl.multiple_of((qi * heads + g) * HD, HD), HD)] for g in range(heads)
         ], axis=0)
-        qpos = qpos_ref[:, pl.ds(r0, TQ)]
-        lo = lo_ref[:, pl.ds(r0, TQ)]
+        qpos = jnp.concatenate([qpos_ref[...]] * heads, axis=1)
+        lo = jnp.concatenate([lo_ref[...]] * heads, axis=1)
         m_sc[...] = jnp.full(m_sc.shape, NEG_FILL, jnp.float32)
         l_sc[...] = jnp.zeros(l_sc.shape, jnp.float32)
         acc_sc[...] = jnp.zeros(acc_sc.shape, jnp.float32)
@@ -348,8 +348,8 @@
     doc_start = jnp.max(jnp.where(doc_ends[None, :] <= pos[:, None], doc_ends[None, :], 0), axis=1)
     block_lo = lax.dynamic_slice_in_dim(mask_lo, here * (row_count // BLK), row_count // BLK)
     lo_tok = jnp.maximum(jnp.repeat(block_lo, BLK) * BLK, doc_start)
-    qpos_rows = jnp.tile(pos, group_size)[None, :]
-    lo_rows = jnp.tile(lo_tok, group_size)[None, :]
+    qpos_rows = pos[None, :]
+    lo_rows = lo_tok[None, :]
     n_q = row_count * group_size // TQ
     tile_lo = jnp.full((n_q,), jnp.min(lo_tok))
     tile_hi = jnp.full((n_q,), pos[-1])

time: 102 us -> 100 us (0.980)
  local copies, waits for them, and re-layouts: 5.06 us -> 3.89 us
    unnamed x5 -> x1, local copies, waits for them, and re-layouts: 2.89 us -> 1.67 us
    pallas_call x1, Pallas kernels: 26.3 us -> 25.2 us  [attend(): pl.pallas_call(functools.partial(attn_kernel, plane, slots), out_shape=ja...]
where the time goes in v1:
time: 100 us; the launch traced here: 99.4 us
  Pallas kernels  90.5 us (90%)
  local copies, waits for them, and re-layouts  3.89 us (4%)
  between operations  2.68 us (3%)
  other arithmetic  2.33 us (2%)
    pallas_call x1, Pallas kernels, gather_window(): pl.pallas_call(functools.partial(window_kernel, depth, plane, n_ctx, need...  33.8 us
    pallas_call x1, Pallas kernels, project(): pl.pallas_call(functools.partial(project_kernel, n_head), out_shape=jax.S...  31.4 us
    pallas_call x1, Pallas kernels, attend(): pl.pallas_call(functools.partial(attn_kernel, plane, slots), out_shape=ja...  25.2 us

profile of v1, /device:TPU:192, one launch (start us, length us, event | category | flops | bytes accessed | tf_op | source)
XLA Modules:
  0.0 99.4 jit_solution(16574208318311062386)
XLA Ops:
  0.0 0.8 dynamic-slice_multiply_fusion
  0.8 0.7 fusion
  2.8 0.7 copy.9
  3.6 0.1 reduce.8
  3.7 0.1 select_reduce_fusion
  3.8 0.1 broadcast_in_dim.16
  3.9 0.1 mul.36
  4.0 0.1 broadcast_in_dim.17
  4.1 0.6 maximum_reduce_fusion
  6.0 0.1 add_add_fusion
  6.1 0.6 maximum_subtract_fusion
  6.7 0.6 broadcast.347.tiles_ref
  7.2 33.8 %shard_map.64 = bf16[4,6,2,256,128]{4,3,2,1,0:T(8,128)(2,1)} custom-call(bf16[256,128]{1,0:T(8,128)(2,1)} %k_ref.1, bf16[256,128]{1,0:T(8,128)(2,1)} %v_ref.1), custom_call_target="tpu_custom_call" | custom-call | tf_op jit(solution)/shard_map/pallas_call | solution.py:243
  41.1 25.2 %shard_map.65.att_ref = bf16[256,1024]{1,0:T(8,128)(2,1)} custom-call(s32[2,4]{1,0:T(2,128)} %broadcast.347.tiles_ref, bf16[256,1024]{1,0:T(8,128)(2,1)} %q_ref.1, bf16[12288,128]{1,0:T(8,128)(2,1)} %bitcast.9, s32[1,256]{1,0:T(1,128)} %get-tuple-element.10.qpos_ref, s32[1,256]{1,0:T(1,128)} %get-tuple-element.9.lo_ref), custom_call_target="tpu_custom_call" | custom-call | tf_op jit(solution)/shard_map/pallas_call | solution.py:92
  66.3 31.4 %shard_map.66 = bf16[256,512]{1,0:T(8,128)(2,1)} custom-call(bf16[256,1024]{1,0:T(8,128)(2,1)} %shard_map.65.att_ref, bf16[1024,4096]{1,0:T(8,128)(2,1)} %w_hbm.1), custom_call_target="tpu_custom_call" | custom-call | tf_op jit(solution)/shard_map/pallas_call | solution.py:324
  97.7 1.7 %copy.11 = bf16[256,512]{1,0:T(8,128)(2,1)} copy(bf16[256,512]{1,0:T(8,128)(2,1)} %shard_map.66) | data formatting | bytes 524288
  (2 shorter events, 0.0 us)
